TPU v7x, 32 devices: a whole 2x2x4 slice. The times are simulated.
32 devices in a mesh: lon: 8 (over y, x, core), lat: 4 (over z).
Axes of the slice: x: 2, y: 2, z: 4, core: 2. Of those that a mesh axis runs over, the one named last changes fastest.
Arguments:
- gradient: float32 [137, 16, 1024], P(None, 'lat', 'lon'), may hold values from -60 to 60
- obs_weight: float32 [137, 16, 1024], P(None, 'lat', 'lon'), may hold values from 0.2 to 5
- half_width: int32 [16], P('lat'), may hold values from 8 to 32
- zonal_coef: float32 [16, 33], P('lat'), may hold values from 0.2 to 1
- mirror_map: int32 [1024], P('lon'), may hold values from 0 to 1023, as said below
- merid_coef: float32 [5], replicated, may hold values from 0.2 to 1
- vertical_map: float32 [137, 137], replicated, may hold values from -0.5 to 0.5
Outputs:
- increment: float32 [137, 16, 1024], P(None, 'lat', 'lon')
- residual: float32 [137, 16, 1024], P(None, 'lat', 'lon')
Inputs may be any that keep to these rules, and one draw needn't show every extreme that they name: mirror_map[mirror_map[i]] = i, and mirror_map[i] lies in the block of 128 longitudes whose block index differs from i // 128 by 4.
All inputs are finite; a program needn't handle non-finite values.
Results may differ from a plain program's by a relative error of at most 0.04.
Values sent between devices are 32-bit elements; how exact they have to be, the bound alone decides.
No kernel may reach another device: no remote copies, remote signals or barrier semaphores. Data moves between devices by JAX's collectives and lax.ppermute only.
A program may use at most 64 MiB of HBM per device.

v0:
```python
import jax
import jax.numpy as jnp
from jax import lax
from jax.sharding import PartitionSpec as P

OUTER = 2


def extended_2(block, sides, width, periodic):
    for axis, dim in sides:
        count = lax.axis_size(axis)
        forward = [(i, i + 1) for i in range(count - 1)]
        if periodic:
            forward.append((count - 1, 0))
        backward = [(target, source) for source, target in forward]
        low = lax.ppermute(
            lax.slice_in_dim(block, block.shape[dim] - width, None, axis=dim), axis, forward
        )
        high = lax.ppermute(lax.slice_in_dim(block, 0, width, axis=dim), axis, backward)
        block = jnp.concatenate([low, block, high], axis=dim)
    return block


def from_partner(value, axis, distance):
    return lax.ppermute(value, axis, [(i, i ^ 1 << distance) for i in range(lax.axis_size(axis))])


def zonal_weights(half_width, zonal_coef):
    tap_ids = jnp.arange(zonal_coef.shape[1], dtype=jnp.int32)
    kept = jnp.where(
        tap_ids[None, :] <= half_width[:, None], zonal_coef, jnp.zeros_like(zonal_coef)
    )
    scaling = jnp.sqrt(kept[:, 0] ** 2 + 2.0 * jnp.sum(kept[:, 1:] ** 2, axis=1))
    return kept / scaling[:, None]


def merid_weights(merid_coef):
    norm_value = jnp.sqrt(merid_coef[0] ** 2 + 2.0 * jnp.sum(merid_coef[1:] ** 2))
    return merid_coef / norm_value


def zonal_tables(weights, lon_dev):
    width = weights.shape[1] - 1
    positions = jnp.arange(lon_dev + 2 * width, dtype=jnp.int32)
    columns = jnp.arange(lon_dev, dtype=jnp.int32)
    tap_ids = jnp.arange(width + 1, dtype=jnp.int32)
    distance = jnp.abs(positions[:, None] - width - columns[None, :])
    selector = (distance[:, :, None] == tap_ids[None, None, :]).astype(jnp.float32)
    return jnp.einsum("pct,jt->jpc", selector, weights, precision=lax.Precision.HIGHEST)


def zonal_apply(padded, table):
    return jnp.einsum("ljp,jpc->ljc", padded, table, precision=lax.Precision.HIGHEST)


def lon_rim(field_in, width):
    return extended_2(field_in, (("lon", 2),), width, True)


def edge_rows(field_in):
    return jnp.concatenate([field_in, field_in], axis=1)


def merid_apply(field_in, polar, mirror_local, weights):
    rim_depth = weights.shape[0] - 1
    row_count = field_in.shape[1]
    extended = extended_2(field_in, (("lat", 1),), rim_depth, False)
    mirrored = jnp.take(polar, mirror_local, axis=2)
    north_rows = jnp.flip(mirrored[:, :rim_depth], axis=1)
    south_rows = jnp.flip(mirrored[:, rim_depth:], axis=1)
    band_index = lax.axis_index("lat")
    band_count = lax.axis_size("lat")
    upper_rim = jnp.where(band_index == 0, north_rows, extended[:, :rim_depth])
    lower_rim = jnp.where(
        band_index == band_count - 1, south_rows, extended[:, rim_depth + row_count :]
    )
    full_rows = jnp.concatenate([upper_rim, field_in, lower_rim], axis=1)
    result = weights[0] * field_in
    for offset in range(1, rim_depth + 1):
        upper = full_rows[:, rim_depth - offset : rim_depth - offset + row_count]
        lower = full_rows[:, rim_depth + offset : rim_depth + offset + row_count]
        result = result + weights[offset] * (upper + lower)
    return result


def per_device(gradient, obs_weight, half_width, zonal_coef, mirror_map, merid_coef, vertical_map):
    width = zonal_coef.shape[1] - 1
    lon_dev = gradient.shape[2]
    zonal_w = zonal_weights(half_width, zonal_coef)
    merid_w = merid_weights(merid_coef)
    table = zonal_tables(zonal_w, lon_dev)
    mirror_local = mirror_map % lon_dev
    partner_bit = lax.axis_size("lon").bit_length() - 2

    def hessian(vector):
        padded = lon_rim(vector, width)
        zonal_out = zonal_apply(padded, table)
        polar = from_partner(edge_rows(zonal_out), "lon", partner_bit)
        forward = merid_apply(zonal_out, polar, mirror_local, merid_w)
        lifted = jnp.einsum("kl,lji->kji", vertical_map, forward, precision=lax.Precision.HIGHEST)
        lowered = jnp.einsum(
            "lk,lji->kji", vertical_map, obs_weight * lifted, precision=lax.Precision.HIGHEST
        )
        returned = from_partner(edge_rows(lowered), "lon", partner_bit)
        merid_back = merid_apply(lowered, returned, mirror_local, merid_w)
        back = zonal_apply(lon_rim(merid_back, width), table)
        return vector + back

    increment = jnp.zeros_like(gradient)
    residual = gradient
    for outer in range(OUTER):
        first = hessian(residual)
        sum_rr, sum_rf, sum_ff = lax.psum(
            (jnp.sum(residual * residual), jnp.sum(residual * first), jnp.sum(first * first)),
            ("lon", "lat"),
        )
        second = hessian(first)
        sum_fs = lax.psum(jnp.sum(first * second), ("lon", "lat"))
        determinant = sum_rf * sum_fs - sum_ff * sum_ff
        coef_one = (sum_fs * sum_rr - sum_ff * sum_rf) / determinant
        coef_two = (sum_rf * sum_rf - sum_ff * sum_rr) / determinant
        increment = increment + coef_one * residual + coef_two * first
        residual = residual - coef_one * first - coef_two * second
    return (increment, residual)


def solution(mesh):
    placed = (
        P(None, "lat", "lon"),
        P(None, "lat", "lon"),
        P("lat"),
        P("lat", None),
        P("lon"),
        P(),
        P(),
    )
    return jax.shard_map(
        per_device,
        mesh=mesh,
        in_specs=placed,
        out_specs=(P(None, "lat", "lon"), P(None, "lat", "lon")),
        check_vma=False,
    )
```

profile of v0, /device:TPU:0, one launch (start us, length us, event | category | flops | bytes accessed | tf_op | source)
XLA Modules:
  0.0 374.2 jit_solution(15704041245719016282)
XLA Ops:
  2.3 2.9 collective-permute-start.1
  5.9 1.3 fusion
  8.6 1.5 collective-permute-done
  10.1 1.5 collective-permute-done.1
  12.7 2.7 collective-permute-start.2
  16.1 4.2 %collective-permute-start.3 = (f32[137,4,128]{2,0,1:T(8,128)S(1)}, f32[137,4,128]{2,0,1:T(8,128)}, u32[]{:S(2)}, u32[]{:S(2)}) collective-permute-start(f32[137,4,128]{2,0,1:T(8,128)S(1)} %convolution_bitcast_fusion.15), channel_id=1, source_target_pairs={{0,1},{1,2},{2,3},{4,5},{5,6},{6,7},{8,9},{9,10},{10,11},{12,13},{... | collective-permute-start | bytes 841736 | tf_op jit(solution)/shard_map/ppermute | solution.py:16
  20.3 1.3 collective-permute-start.4
  21.6 7.2 %collective-permute-done.2 = f32[137,8,128]{2,1,0:T(8,128)S(1)} collective-permute-done((f32[137,8,128]{2,1,0:T(8,128)S(1)}, f32[137,8,128]{2,1,0:T(8,128)S(1)}, u32[]{:S(2)}, u32[]{:S(2)}) %collective-permute-start.2) | collective-permute-done | bytes 561184 | tf_op jit(solution)/shard_map/ppermute | solution.py:25
  31.7 3.9 %fusion.5 = f32[137,4,128]{2,0,1:T(8,128)S(1)} fusion(f32[137,4,128]{2,0,1:T(8,128)S(1)} %reverse_select_fusion.14, f32[137,4,128]{2,0,1:T(8,128)S(1)} %reverse_select_fusion.15, f32[137,4,128]{2,0,1:T(8,128)S(1)} %convolution_bitcast_fusion.15, f32[137,4,128]{2,1,0:T(4,128)S(1)} %copy-done.4, f32[137,137]{1,0:T(8,128)S(1)} %copy-done, f32[]{:T(128)} %bitcast.9, ...), kind=kOutput, calls=%fused_computation.29 | convolution fusion | flops 116719616 | bytes 1477976 | tf_op jit(solution)/shard_map/kl,lji->kji/dot_general | solution.py:100
  37.6 5.3 %collective-permute-start.6 = (f32[137,4,128]{2,0,1:T(8,128)S(1)}, f32[137,4,128]{2,0,1:T(8,128)}, u32[]{:S(2)}, u32[]{:S(2)}) collective-permute-start(f32[137,4,128]{2,0,1:T(8,128)S(1)} %convolution_bitcast_fusion.13), channel_id=1, source_target_pairs={{0,1},{1,2},{2,3},{4,5},{5,6},{6,7},{8,9},{9,10},{10,11},{12,13},{... | collective-permute-start | bytes 841736 | tf_op jit(solution)/shard_map/ppermute | solution.py:16
  42.9 1.3 collective-permute-start.7
  44.2 7.4 %collective-permute-done.5 = f32[137,8,128]{2,1,0:T(8,128)S(1)} collective-permute-done((f32[137,8,128]{2,1,0:T(8,128)S(1)}, f32[137,8,128]{2,1,0:T(8,128)S(1)}, u32[]{:S(2)}, u32[]{:S(2)}) %collective-permute-start.5) | collective-permute-done | bytes 561184 | tf_op jit(solution)/shard_map/ppermute | solution.py:25
  53.5 3.5 fusion.139
  57.2 2.6 collective-permute-start.9
  59.8 7.0 %collective-permute-done.8 = f32[137,4,32]{2,0,1:T(8,128)S(1)} collective-permute-done((f32[137,4,32]{2,0,1:T(8,128)S(1)}, f32[137,4,32]{2,0,1:T(8,128)S(1)}, u32[]{:S(2)}, u32[]{:S(2)}) %collective-permute-start.8) | collective-permute-done | bytes 70176 | tf_op jit(solution)/shard_map/ppermute | solution.py:16
  67.9 2.5 collective-permute-start.11
  70.5 7.3 %collective-permute-done.10 = f32[137,4,32]{2,0,1:T(8,128)S(1)} collective-permute-done((f32[137,4,32]{2,0,1:T(8,128)S(1)}, f32[137,4,32]{2,0,1:T(8,128)S(1)}, u32[]{:S(2)}, u32[]{:S(2)}) %collective-permute-start.10) | collective-permute-done | bytes 70176 | tf_op jit(solution)/shard_map/ppermute | solution.py:16
  79.5 5.6 %collective-permute-start.13 = (f32[137,4,128]{2,0,1:T(8,128)S(1)}, f32[137,4,128]{2,0,1:T(8,128)}, u32[]{:S(2)}, u32[]{:S(2)}) collective-permute-start(f32[137,4,128]{2,0,1:T(8,128)S(1)} %convolution_bitcast_fusion.11), channel_id=1, source_target_pairs={{0,1},{1,2},{2,3},{4,5},{5,6},{6,7},{8,9},{9,10},{10,11},{12,13},{... | collective-permute-start | bytes 841736 | tf_op jit(solution)/shard_map/ppermute | solution.py:16
  85.1 1.5 collective-permute-start.14
  86.6 6.5 %collective-permute-done.12 = f32[137,8,128]{2,1,0:T(8,128)S(1)} collective-permute-done((f32[137,8,128]{2,1,0:T(8,128)S(1)}, f32[137,8,128]{2,1,0:T(8,128)S(1)}, u32[]{:S(2)}, u32[]{:S(2)}) %collective-permute-start.12) | collective-permute-done | bytes 561184 | tf_op jit(solution)/shard_map/ppermute | solution.py:25
  96.4 3.9 %fusion.4 = f32[137,4,128]{2,0,1:T(8,128)S(1)} fusion(f32[137,4,128]{2,0,1:T(8,128)S(1)} %reverse_select_fusion.10, f32[137,4,128]{2,0,1:T(8,128)S(1)} %reverse_select_fusion.11, f32[137,4,128]{2,0,1:T(8,128)S(1)} %convolution_bitcast_fusion.11, f32[137,4,128]{2,1,0:T(4,128)S(1)} %copy-done.5, f32[137,137]{1,0:T(8,128)S(1)} %copy-done, f32[]{:T(128)} %bitcast.9, ...), kind=kOutput, calls=%fused_computation.24 | convolution fusion | flops 116719616 | bytes 1477976 | tf_op jit(solution)/shard_map/kl,lji->kji/dot_general | solution.py:100
  101.7 6.7 %collective-permute-start.16 = (f32[137,4,128]{2,0,1:T(8,128)S(1)}, f32[137,4,128]{2,0,1:T(8,128)}, u32[]{:S(2)}, u32[]{:S(2)}) collective-permute-start(f32[137,4,128]{2,0,1:T(8,128)S(1)} %convolution_bitcast_fusion.9), channel_id=1, source_target_pairs={{0,1},{1,2},{2,3},{4,5},{5,6},{6,7},{8,9},{9,10},{10,11},{12,13},{... | collective-permute-start | bytes 841736 | tf_op jit(solution)/shard_map/ppermute | solution.py:16
  109.7 4.6 %collective-permute-done.15 = f32[137,8,128]{2,1,0:T(8,128)S(1)} collective-permute-done((f32[137,8,128]{2,1,0:T(8,128)S(1)}, f32[137,8,128]{2,1,0:T(8,128)S(1)}, u32[]{:S(2)}, u32[]{:S(2)}) %collective-permute-start.15) | collective-permute-done | bytes 561184 | tf_op jit(solution)/shard_map/ppermute | solution.py:25
  116.2 1.8 collective-permute-done.17
  118.9 3.4 fusion.111
  122.6 2.6 collective-permute-start.19
  126.0 6.3 %collective-permute-done.18 = f32[137,4,32]{2,0,1:T(8,128)S(1)} collective-permute-done((f32[137,4,32]{2,0,1:T(8,128)S(1)}, f32[137,4,32]{2,0,1:T(8,128)S(1)}, u32[]{:S(2)}, u32[]{:S(2)}) %collective-permute-start.18) | collective-permute-done | bytes 70176 | tf_op jit(solution)/shard_map/ppermute | solution.py:16
  132.3 1.5 multiply_reduce_fusion.6
  133.8 40.9 %all-reduce.1 = (f32[]{:T(128)}, f32[]{:T(128)}, f32[]{:T(128)}, f32[]{:T(128)}) all-reduce(f32[]{:T(128)} %get-tuple-element.18, f32[]{:T(128)} %get-tuple-element.19, f32[]{:T(128)} %multiply_reduce_fusion.7, f32[]{:T(128)} %get-tuple-element.17), channel_id=1, replica_groups=mesh['lon'=8,'lat'=4] {'lon','lat'}, use_global_device_ids=true, to_apply=%region_9.11 | all-reduce | flops 4 | bytes 32 | tf_op jit(solution)/shard_map/psum | solution.py:113
  182.6 2.6 collective-permute-start.21
  185.3 4.5 %collective-permute-done.20 = f32[137,4,32]{2,0,1:T(8,128)S(1)} collective-permute-done((f32[137,4,32]{2,0,1:T(8,128)S(1)}, f32[137,4,32]{2,0,1:T(8,128)S(1)}, u32[]{:S(2)}, u32[]{:S(2)}) %collective-permute-start.20) | collective-permute-done | bytes 70176 | tf_op jit(solution)/shard_map/ppermute | solution.py:16
  189.8 2.0 collective-permute-done.21
  191.7 1.5 convolution_bitcast_fusion.7
  194.5 3.1 collective-permute-start.22
  197.6 2.6 collective-permute-start.23
  201.5 9.7 %collective-permute-done.22 = f32[137,8,128]{2,1,0:T(8,128)S(1)} collective-permute-done((f32[137,8,128]{2,1,0:T(8,128)S(1)}, f32[137,8,128]{2,1,0:T(8,128)S(1)}, u32[]{:S(2)}, u32[]{:S(2)}) %collective-permute-start.22) | collective-permute-done | bytes 561184 | tf_op jit(solution)/shard_map/ppermute | solution.py:25
  214.1 5.3 %fusion.3 = f32[137,4,128]{2,0,1:T(8,128)S(1)} fusion(f32[137,4,128]{2,0,1:T(8,128)S(1)} %reverse_select_fusion.6, f32[137,4,128]{2,0,1:T(8,128)S(1)} %reverse_select_fusion.7, f32[137,4,128]{2,0,1:T(8,128)} %convolution_bitcast_fusion.7, f32[137,4,128]{2,1,0:T(4,128)S(1)} %copy-done.6, f32[137,137]{1,0:T(8,128)S(1)} %copy-done, f32[]{:T(128)} %bitcast.9, ...), kind=kOutput, calls=%fused_computation.19 | convolution fusion | flops 116719616 | bytes 1477976 | tf_op jit(solution)/shard_map/kl,lji->kji/dot_general | solution.py:100
  220.6 3.5 collective-permute-start.26
  224.2 1.5 collective-permute-start.27
  225.7 9.4 %collective-permute-done.25 = f32[137,8,128]{2,1,0:T(8,128)S(1)} collective-permute-done((f32[137,8,128]{2,1,0:T(8,128)S(1)}, f32[137,8,128]{2,1,0:T(8,128)S(1)}, u32[]{:S(2)}, u32[]{:S(2)}) %collective-permute-start.25) | collective-permute-done | bytes 561184 | tf_op jit(solution)/shard_map/ppermute | solution.py:25
  235.6 1.7 gather_fusion.5
  237.3 1.6 copy.216
  240.1 3.4 fusion.83
  243.7 2.6 collective-permute-start.29
  246.3 7.2 %collective-permute-done.28 = f32[137,4,32]{2,0,1:T(8,128)S(1)} collective-permute-done((f32[137,4,32]{2,0,1:T(8,128)S(1)}, f32[137,4,32]{2,0,1:T(8,128)S(1)}, u32[]{:S(2)}, u32[]{:S(2)}) %collective-permute-start.28) | collective-permute-done | bytes 70176 | tf_op jit(solution)/shard_map/ppermute | solution.py:16
  254.6 2.6 collective-permute-start.31
  257.2 7.1 %collective-permute-done.30 = f32[137,4,32]{2,0,1:T(8,128)S(1)} collective-permute-done((f32[137,4,32]{2,0,1:T(8,128)S(1)}, f32[137,4,32]{2,0,1:T(8,128)S(1)}, u32[]{:S(2)}, u32[]{:S(2)}) %collective-permute-start.30) | collective-permute-done | bytes 70176 | tf_op jit(solution)/shard_map/ppermute | solution.py:16
  265.5 4.5 %collective-permute-start.33 = (f32[137,4,128]{2,0,1:T(8,128)S(1)}, f32[137,4,128]{2,0,1:T(8,128)}, u32[]{:S(2)}, u32[]{:S(2)}) collective-permute-start(f32[137,4,128]{2,0,1:T(8,128)S(1)} %convolution_bitcast_fusion.3), channel_id=1, source_target_pairs={{0,1},{1,2},{2,3},{4,5},{5,6},{6,7},{8,9},{9,10},{10,11},{12,13},{... | collective-permute-start | bytes 841736 | tf_op jit(solution)/shard_map/ppermute | solution.py:16
  271.2 7.6 %collective-permute-done.32 = f32[137,8,128]{2,1,0:T(8,128)} collective-permute-done((f32[137,8,128]{2,1,0:T(8,128)S(1)}, f32[137,8,128]{2,1,0:T(8,128)}, u32[]{:S(2)}, u32[]{:S(2)}) %collective-permute-start.32) | collective-permute-done | bytes 561184 | tf_op jit(solution)/shard_map/ppermute | solution.py:25
  278.9 1.6 copy.220
  280.4 1.7 gather_fusion.6
  282.2 1.6 copy.221
  284.8 3.9 %fusion.2 = f32[137,4,128]{2,0,1:T(8,128)S(1)} fusion(f32[137,4,128]{2,0,1:T(8,128)S(1)} %reverse_select_fusion.2, f32[137,4,128]{2,0,1:T(8,128)S(1)} %reverse_select_fusion.3, f32[137,4,128]{2,0,1:T(8,128)S(1)} %convolution_bitcast_fusion.3, f32[137,4,128]{2,1,0:T(4,128)S(1)} %copy-done.7, f32[137,137]{1,0:T(8,128)S(1)} %copy-done, f32[]{:T(128)} %bitcast.9, ...), kind=kOutput, calls=%fused_computation.14 | convolution fusion | flops 116719616 | bytes 1477976 | tf_op jit(solution)/shard_map/kl,lji->kji/dot_general | solution.py:100
  289.5 1.4 collective-permute-start.35
  290.9 4.9 %collective-permute-start.36 = (f32[137,4,128]{2,0,1:T(8,128)S(1)}, f32[137,4,128]{2,0,1:T(8,128)}, u32[]{:S(2)}, u32[]{:S(2)}) collective-permute-start(f32[137,4,128]{2,0,1:T(8,128)S(1)} %convolution_bitcast_fusion.1), channel_id=1, source_target_pairs={{0,1},{1,2},{2,3},{4,5},{5,6},{6,7},{8,9},{9,10},{10,11},{12,13},{... | collective-permute-start | bytes 841736 | tf_op jit(solution)/shard_map/ppermute | solution.py:16
  297.1 6.0 %collective-permute-done.35 = f32[137,8,128]{2,1,0:T(8,128)} collective-permute-done((f32[137,8,128]{2,1,0:T(8,128)S(1)}, f32[137,8,128]{2,1,0:T(8,128)}, u32[]{:S(2)}, u32[]{:S(2)}) %collective-permute-start.35) | collective-permute-done | bytes 561184 | tf_op jit(solution)/shard_map/ppermute | solution.py:25
  303.1 1.6 copy.225
  304.6 1.7 gather_fusion.7
  306.4 1.6 copy.226
  308.2 3.4 fusion.55
  311.8 2.6 collective-permute-start.39
  314.4 5.4 %collective-permute-done.38 = f32[137,4,32]{2,0,1:T(8,128)S(1)} collective-permute-done((f32[137,4,32]{2,0,1:T(8,128)S(1)}, f32[137,4,32]{2,0,1:T(8,128)S(1)}, u32[]{:S(2)}, u32[]{:S(2)}) %collective-permute-start.38) | collective-permute-done | bytes 70176 | tf_op jit(solution)/shard_map/ppermute | solution.py:16
  320.3 1.5 multiply_reduce_fusion.3
  321.8 42.7 %all-reduce = (f32[]{:T(128)}, f32[]{:T(128)}, f32[]{:T(128)}, f32[]{:T(128)}) all-reduce(f32[]{:T(128)} %get-tuple-element.14, f32[]{:T(128)} %get-tuple-element.16, f32[]{:T(128)} %get-tuple-element.15, f32[]{:T(128)} %get-tuple-element.13), channel_id=1, replica_groups=mesh['lon'=8,'lat'=4] {'lon','lat'}, use_global_device_ids=true, to_apply=%region_17.19 | all-reduce | flops 4 | bytes 32 | tf_op jit(solution)/shard_map/psum | solution.py:113
  (157 shorter events, 42.2 us)
Async XLA Ops:
  0.6 31.1 %copy-start = (f32[137,137]{1,0:T(8,128)S(1)}, f32[137,137]{1,0:T(8,128)}, u32[]{:S(2)}) copy-start(f32[137,137]{1,0:T(8,128)} %param.15) | copy-start | bytes 225232
  0.6 4.6 %copy-start.3 = (s32[4]{0:T(128)S(1)}, s32[4]{0:T(128)}, u32[]{:S(2)}) copy-start(s32[4]{0:T(128)} %param.11) | copy-start | bytes 52
  0.7 4.6 %copy-start.2 = (f32[4,33]{1,0:T(4,128)S(1)}, f32[4,33]{1,0:T(4,128)}, u32[]{:S(2)}) copy-start(f32[4,33]{1,0:T(4,128)} %param.12) | copy-start | bytes 1588
  0.7 5.2 %copy-start.9 = (f32[5]{0:T(128)S(1)}, f32[5]{0:T(128)}, u32[]{:S(2)}) copy-start(f32[5]{0:T(128)} %param.14) | copy-start | bytes 64
  1.8 8.3 %collective-permute-start = (f32[137,4,32]{2,0,1:T(8,128)S(1)}, f32[137,4,32]{2,0,1:T(8,128)S(1)}, u32[]{:S(2)}, u32[]{:S(2)}) collective-permute-start(f32[137,4,32]{2,0,1:T(8,128)S(1)} %get-tuple-element.62), channel_id=1, source_target_pairs={{0,4},{4,8},{8,12},{12,16},{16,20},{20,24},{24,28},{28,0},{1,5},{5... | collective-permute-start | bytes 210440 | tf_op jit(solution)/shard_map/ppermute | solution.py:16
  2.3 9.3 %collective-permute-start.1 = (f32[137,4,32]{2,0,1:T(8,128)S(1)}, f32[137,4,32]{2,0,1:T(8,128)S(1)}, u32[]{:S(2)}, u32[]{:S(2)}) collective-permute-start(f32[137,4,32]{2,0,1:T(8,128)S(1)} %get-tuple-element.63), channel_id=1, source_target_pairs={{4,0},{8,4},{12,8},{16,12},{20,16},{24,20},{28,24},{0,28},{5,1},{9... | collective-permute-start | bytes 210440 | tf_op jit(solution)/shard_map/ppermute | solution.py:19
  12.5 2.9 copy-start.8
  12.7 16.0 %collective-permute-start.2 = (f32[137,8,128]{2,1,0:T(8,128)S(1)}, f32[137,8,128]{2,1,0:T(8,128)S(1)}, u32[]{:S(2)}, u32[]{:S(2)}) collective-permute-start(f32[137,8,128]{2,1,0:T(8,128)S(1)} %copy.185), channel_id=1, source_target_pairs={{0,16},{4,20},{8,24},{12,28},{16,0},{20,4},{24,8},{28,12},{1,17},{... | collective-permute-start | bytes 1683464 | tf_op jit(solution)/shard_map/ppermute | solution.py:25
  16.1 14.5 %collective-permute-start.3 = (f32[137,4,128]{2,0,1:T(8,128)S(1)}, f32[137,4,128]{2,0,1:T(8,128)}, u32[]{:S(2)}, u32[]{:S(2)}) collective-permute-start(f32[137,4,128]{2,0,1:T(8,128)S(1)} %convolution_bitcast_fusion.15), channel_id=1, source_target_pairs={{0,1},{1,2},{2,3},{4,5},{5,6},{6,7},{8,9},{9,10},{10,11},{12,13},{... | collective-permute-start | bytes 841736 | tf_op jit(solution)/shard_map/ppermute | solution.py:16
  20.3 10.4 %collective-permute-start.4 = (f32[137,4,128]{2,0,1:T(8,128)S(1)}, f32[137,4,128]{2,0,1:T(8,128)}, u32[]{:S(2)}, u32[]{:S(2)}) collective-permute-start(f32[137,4,128]{2,0,1:T(8,128)S(1)} %convolution_bitcast_fusion.15), channel_id=1, source_target_pairs={{1,0},{2,1},{3,2},{5,4},{6,5},{7,6},{9,8},{10,9},{11,10},{13,12},{... | collective-permute-start | bytes 841736 | tf_op jit(solution)/shard_map/ppermute | solution.py:19
  30.6 1.1 copy-start.4
  36.4 15.1 %collective-permute-start.5 = (f32[137,8,128]{2,1,0:T(8,128)S(1)}, f32[137,8,128]{2,1,0:T(8,128)S(1)}, u32[]{:S(2)}, u32[]{:S(2)}) collective-permute-start(f32[137,8,128]{2,1,0:T(8,128)S(1)} %copy.190), channel_id=1, source_target_pairs={{0,16},{4,20},{8,24},{12,28},{16,0},{20,4},{24,8},{28,12},{1,17},{... | collective-permute-start | bytes 1683464 | tf_op jit(solution)/shard_map/ppermute | solution.py:25
  37.6 15.8 %collective-permute-start.6 = (f32[137,4,128]{2,0,1:T(8,128)S(1)}, f32[137,4,128]{2,0,1:T(8,128)}, u32[]{:S(2)}, u32[]{:S(2)}) collective-permute-start(f32[137,4,128]{2,0,1:T(8,128)S(1)} %convolution_bitcast_fusion.13), channel_id=1, source_target_pairs={{0,1},{1,2},{2,3},{4,5},{5,6},{6,7},{8,9},{9,10},{10,11},{12,13},{... | collective-permute-start | bytes 841736 | tf_op jit(solution)/shard_map/ppermute | solution.py:16
  42.9 10.6 %collective-permute-start.7 = (f32[137,4,128]{2,0,1:T(8,128)S(1)}, f32[137,4,128]{2,0,1:T(8,128)S(1)}, u32[]{:S(2)}, u32[]{:S(2)}) collective-permute-start(f32[137,4,128]{2,0,1:T(8,128)S(1)} %convolution_bitcast_fusion.13), channel_id=1, source_target_pairs={{1,0},{2,1},{3,2},{5,4},{6,5},{7,6},{9,8},{10,9},{11,10},{13,12},{... | collective-permute-start | bytes 841736 | tf_op jit(solution)/shard_map/ppermute | solution.py:19
  53.5 13.3 %copy-start.1 = (f32[137,4,128]{2,1,0:T(4,128)S(1)}, f32[137,4,128]{2,1,0:T(4,128)}, u32[]{:S(2)}) copy-start(f32[137,4,128]{2,1,0:T(4,128)} %param.9) | copy-start | bytes 841732
  57.1 9.7 %collective-permute-start.8 = (f32[137,4,32]{2,0,1:T(8,128)S(1)}, f32[137,4,32]{2,0,1:T(8,128)S(1)}, u32[]{:S(2)}, u32[]{:S(2)}) collective-permute-start(f32[137,4,32]{2,0,1:T(8,128)S(1)} %get-tuple-element.60), channel_id=1, source_target_pairs={{0,4},{4,8},{8,12},{12,16},{16,20},{20,24},{24,28},{28,0},{1,5},{5... | collective-permute-start | bytes 210440 | tf_op jit(solution)/shard_map/ppermute | solution.py:16
  57.2 9.6 %collective-permute-start.9 = (f32[137,4,32]{2,0,1:T(8,128)S(1)}, f32[137,4,32]{2,0,1:T(8,128)S(1)}, u32[]{:S(2)}, u32[]{:S(2)}) collective-permute-start(f32[137,4,32]{2,0,1:T(8,128)S(1)} %get-tuple-element.61), channel_id=1, source_target_pairs={{4,0},{8,4},{12,8},{16,12},{20,16},{24,20},{28,24},{0,28},{5,1},{9... | collective-permute-start | bytes 210440 | tf_op jit(solution)/shard_map/ppermute | solution.py:19
  67.8 10.0 %collective-permute-start.10 = (f32[137,4,32]{2,0,1:T(8,128)S(1)}, f32[137,4,32]{2,0,1:T(8,128)S(1)}, u32[]{:S(2)}, u32[]{:S(2)}) collective-permute-start(f32[137,4,32]{2,0,1:T(8,128)S(1)} %get-tuple-element.58), channel_id=1, source_target_pairs={{0,4},{4,8},{8,12},{12,16},{16,20},{20,24},{24,28},{28,0},{1,5},{5... | collective-permute-start | bytes 210440 | tf_op jit(solution)/shard_map/ppermute | solution.py:16
  67.9 9.9 %collective-permute-start.11 = (f32[137,4,32]{2,0,1:T(8,128)S(1)}, f32[137,4,32]{2,0,1:T(8,128)S(1)}, u32[]{:S(2)}, u32[]{:S(2)}) collective-permute-start(f32[137,4,32]{2,0,1:T(8,128)S(1)} %get-tuple-element.59), channel_id=1, source_target_pairs={{4,0},{8,4},{12,8},{16,12},{20,16},{24,20},{28,24},{0,28},{5,1},{9... | collective-permute-start | bytes 210440 | tf_op jit(solution)/shard_map/ppermute | solution.py:19
  78.9 14.2 %collective-permute-start.12 = (f32[137,8,128]{2,1,0:T(8,128)S(1)}, f32[137,8,128]{2,1,0:T(8,128)S(1)}, u32[]{:S(2)}, u32[]{:S(2)}) collective-permute-start(f32[137,8,128]{2,1,0:T(8,128)S(1)} %copy.196), channel_id=1, source_target_pairs={{0,16},{4,20},{8,24},{12,28},{16,0},{20,4},{24,8},{28,12},{1,17},{... | collective-permute-start | bytes 1683464 | tf_op jit(solution)/shard_map/ppermute | solution.py:25
  79.5 15.4 %collective-permute-start.13 = (f32[137,4,128]{2,0,1:T(8,128)S(1)}, f32[137,4,128]{2,0,1:T(8,128)}, u32[]{:S(2)}, u32[]{:S(2)}) collective-permute-start(f32[137,4,128]{2,0,1:T(8,128)S(1)} %convolution_bitcast_fusion.11), channel_id=1, source_target_pairs={{0,1},{1,2},{2,3},{4,5},{5,6},{6,7},{8,9},{9,10},{10,11},{12,13},{... | collective-permute-start | bytes 841736 | tf_op jit(solution)/shard_map/ppermute | solution.py:16
  85.1 10.3 %collective-permute-start.14 = (f32[137,4,128]{2,0,1:T(8,128)S(1)}, f32[137,4,128]{2,0,1:T(8,128)}, u32[]{:S(2)}, u32[]{:S(2)}) collective-permute-start(f32[137,4,128]{2,0,1:T(8,128)S(1)} %convolution_bitcast_fusion.11), channel_id=1, source_target_pairs={{1,0},{2,1},{3,2},{5,4},{6,5},{7,6},{9,8},{10,9},{11,10},{13,12},{... | collective-permute-start | bytes 841736 | tf_op jit(solution)/shard_map/ppermute | solution.py:19
  94.9 1.5 copy-start.5
  101.1 13.2 %collective-permute-start.15 = (f32[137,8,128]{2,1,0:T(8,128)S(1)}, f32[137,8,128]{2,1,0:T(8,128)S(1)}, u32[]{:S(2)}, u32[]{:S(2)}) collective-permute-start(f32[137,8,128]{2,1,0:T(8,128)S(1)} %copy.201), channel_id=1, source_target_pairs={{0,16},{4,20},{8,24},{12,28},{16,0},{20,4},{24,8},{28,12},{1,17},{... | collective-permute-start | bytes 1683464 | tf_op jit(solution)/shard_map/ppermute | solution.py:25
  101.7 14.4 %collective-permute-start.16 = (f32[137,4,128]{2,0,1:T(8,128)S(1)}, f32[137,4,128]{2,0,1:T(8,128)}, u32[]{:S(2)}, u32[]{:S(2)}) collective-permute-start(f32[137,4,128]{2,0,1:T(8,128)S(1)} %convolution_bitcast_fusion.9), channel_id=1, source_target_pairs={{0,1},{1,2},{2,3},{4,5},{5,6},{6,7},{8,9},{9,10},{10,11},{12,13},{... | collective-permute-start | bytes 841736 | tf_op jit(solution)/shard_map/ppermute | solution.py:16
  108.4 9.6 %collective-permute-start.17 = (f32[137,4,128]{2,0,1:T(8,128)S(1)}, f32[137,4,128]{2,0,1:T(8,128)}, u32[]{:S(2)}, u32[]{:S(2)}) collective-permute-start(f32[137,4,128]{2,0,1:T(8,128)S(1)} %convolution_bitcast_fusion.9), channel_id=1, source_target_pairs={{1,0},{2,1},{3,2},{5,4},{6,5},{7,6},{9,8},{10,9},{11,10},{13,12},{... | collective-permute-start | bytes 841736 | tf_op jit(solution)/shard_map/ppermute | solution.py:19
  122.5 9.8 %collective-permute-start.18 = (f32[137,4,32]{2,0,1:T(8,128)S(1)}, f32[137,4,32]{2,0,1:T(8,128)S(1)}, u32[]{:S(2)}, u32[]{:S(2)}) collective-permute-start(f32[137,4,32]{2,0,1:T(8,128)S(1)} %get-tuple-element.56), channel_id=1, source_target_pairs={{0,4},{4,8},{8,12},{12,16},{16,20},{20,24},{24,28},{28,0},{1,5},{5... | collective-permute-start | bytes 210440 | tf_op jit(solution)/shard_map/ppermute | solution.py:16
  122.6 9.7 %collective-permute-start.19 = (f32[137,4,32]{2,0,1:T(8,128)S(1)}, f32[137,4,32]{2,0,1:T(8,128)S(1)}, u32[]{:S(2)}, u32[]{:S(2)}) collective-permute-start(f32[137,4,32]{2,0,1:T(8,128)S(1)} %get-tuple-element.57), channel_id=1, source_target_pairs={{4,0},{8,4},{12,8},{16,12},{20,16},{24,20},{28,24},{0,28},{5,1},{9... | collective-permute-start | bytes 210440 | tf_op jit(solution)/shard_map/ppermute | solution.py:19
  182.6 7.2 %collective-permute-start.20 = (f32[137,4,32]{2,0,1:T(8,128)S(1)}, f32[137,4,32]{2,0,1:T(8,128)S(1)}, u32[]{:S(2)}, u32[]{:S(2)}) collective-permute-start(f32[137,4,32]{2,0,1:T(8,128)S(1)} %get-tuple-element.54), channel_id=1, source_target_pairs={{0,4},{4,8},{8,12},{12,16},{16,20},{20,24},{24,28},{28,0},{1,5},{5... | collective-permute-start | bytes 210440 | tf_op jit(solution)/shard_map/ppermute | solution.py:16
  182.6 9.1 %collective-permute-start.21 = (f32[137,4,32]{2,0,1:T(8,128)S(1)}, f32[137,4,32]{2,0,1:T(8,128)S(1)}, u32[]{:S(2)}, u32[]{:S(2)}) collective-permute-start(f32[137,4,32]{2,0,1:T(8,128)S(1)} %get-tuple-element.55), channel_id=1, source_target_pairs={{4,0},{8,4},{12,8},{16,12},{20,16},{24,20},{28,24},{0,28},{5,1},{9... | collective-permute-start | bytes 210440 | tf_op jit(solution)/shard_map/ppermute | solution.py:19
  194.5 16.6 %collective-permute-start.22 = (f32[137,8,128]{2,1,0:T(8,128)S(1)}, f32[137,8,128]{2,1,0:T(8,128)S(1)}, u32[]{:S(2)}, u32[]{:S(2)}) collective-permute-start(f32[137,8,128]{2,1,0:T(8,128)S(1)} %copy.209), channel_id=1, source_target_pairs={{0,16},{4,20},{8,24},{12,28},{16,0},{20,4},{24,8},{28,12},{1,17},{... | collective-permute-start | bytes 1683464 | tf_op jit(solution)/shard_map/ppermute | solution.py:25
  197.6 15.4 %collective-permute-start.23 = (f32[137,4,128]{2,0,1:T(8,128)}, f32[137,4,128]{2,0,1:T(8,128)}, u32[]{:S(2)}, u32[]{:S(2)}) collective-permute-start(f32[137,4,128]{2,0,1:T(8,128)} %convolution_bitcast_fusion.7), channel_id=1, source_target_pairs={{0,1},{1,2},{2,3},{4,5},{5,6},{6,7},{8,9},{9,10},{10,11},{12,13},{... | collective-permute-start | bytes 841736 | tf_op jit(solution)/shard_map/ppermute | solution.py:16
  200.2 12.9 %collective-permute-start.24 = (f32[137,4,128]{2,0,1:T(8,128)}, f32[137,4,128]{2,0,1:T(8,128)}, u32[]{:S(2)}, u32[]{:S(2)}) collective-permute-start(f32[137,4,128]{2,0,1:T(8,128)} %convolution_bitcast_fusion.7), channel_id=1, source_target_pairs={{1,0},{2,1},{3,2},{5,4},{6,5},{7,6},{9,8},{10,9},{11,10},{13,12},{... | collective-permute-start | bytes 841736 | tf_op jit(solution)/shard_map/ppermute | solution.py:19
  213.0 1.1 copy-start.6
  220.3 14.8 %collective-permute-start.25 = (f32[137,8,128]{2,1,0:T(8,128)S(1)}, f32[137,8,128]{2,1,0:T(8,128)S(1)}, u32[]{:S(2)}, u32[]{:S(2)}) collective-permute-start(f32[137,8,128]{2,1,0:T(8,128)S(1)} %copy.214), channel_id=1, source_target_pairs={{0,16},{4,20},{8,24},{12,28},{16,0},{20,4},{24,8},{28,12},{1,17},{... | collective-permute-start | bytes 1683464 | tf_op jit(solution)/shard_map/ppermute | solution.py:25
  220.6 18.4 %collective-permute-start.26 = (f32[137,4,128]{2,0,1:T(8,128)S(1)}, f32[137,4,128]{2,0,1:T(8,128)}, u32[]{:S(2)}, u32[]{:S(2)}) collective-permute-start(f32[137,4,128]{2,0,1:T(8,128)S(1)} %convolution_bitcast_fusion.5), channel_id=1, source_target_pairs={{0,1},{1,2},{2,3},{4,5},{5,6},{6,7},{8,9},{9,10},{10,11},{12,13},{... | collective-permute-start | bytes 841736 | tf_op jit(solution)/shard_map/ppermute | solution.py:16
  224.2 14.9 %collective-permute-start.27 = (f32[137,4,128]{2,0,1:T(8,128)S(1)}, f32[137,4,128]{2,0,1:T(8,128)}, u32[]{:S(2)}, u32[]{:S(2)}) collective-permute-start(f32[137,4,128]{2,0,1:T(8,128)S(1)} %convolution_bitcast_fusion.5), channel_id=1, source_target_pairs={{1,0},{2,1},{3,2},{5,4},{6,5},{7,6},{9,8},{10,9},{11,10},{13,12},{... | collective-permute-start | bytes 841736 | tf_op jit(solution)/shard_map/ppermute | solution.py:19
  243.6 9.9 %collective-permute-start.28 = (f32[137,4,32]{2,0,1:T(8,128)S(1)}, f32[137,4,32]{2,0,1:T(8,128)S(1)}, u32[]{:S(2)}, u32[]{:S(2)}) collective-permute-start(f32[137,4,32]{2,0,1:T(8,128)S(1)} %get-tuple-element.52), channel_id=1, source_target_pairs={{0,4},{4,8},{8,12},{12,16},{16,20},{20,24},{24,28},{28,0},{1,5},{5... | collective-permute-start | bytes 210440 | tf_op jit(solution)/shard_map/ppermute | solution.py:16
  243.7 9.8 %collective-permute-start.29 = (f32[137,4,32]{2,0,1:T(8,128)S(1)}, f32[137,4,32]{2,0,1:T(8,128)S(1)}, u32[]{:S(2)}, u32[]{:S(2)}) collective-permute-start(f32[137,4,32]{2,0,1:T(8,128)S(1)} %get-tuple-element.53), channel_id=1, source_target_pairs={{4,0},{8,4},{12,8},{16,12},{20,16},{24,20},{28,24},{0,28},{5,1},{9... | collective-permute-start | bytes 210440 | tf_op jit(solution)/shard_map/ppermute | solution.py:19
  254.5 9.8 %collective-permute-start.30 = (f32[137,4,32]{2,0,1:T(8,128)S(1)}, f32[137,4,32]{2,0,1:T(8,128)S(1)}, u32[]{:S(2)}, u32[]{:S(2)}) collective-permute-start(f32[137,4,32]{2,0,1:T(8,128)S(1)} %get-tuple-element.50), channel_id=1, source_target_pairs={{0,4},{4,8},{8,12},{12,16},{16,20},{20,24},{24,28},{28,0},{1,5},{5... | collective-permute-start | bytes 210440 | tf_op jit(solution)/shard_map/ppermute | solution.py:16
  254.6 9.7 %collective-permute-start.31 = (f32[137,4,32]{2,0,1:T(8,128)S(1)}, f32[137,4,32]{2,0,1:T(8,128)S(1)}, u32[]{:S(2)}, u32[]{:S(2)}) collective-permute-start(f32[137,4,32]{2,0,1:T(8,128)S(1)} %get-tuple-element.51), channel_id=1, source_target_pairs={{4,0},{8,4},{12,8},{16,12},{20,16},{24,20},{28,24},{0,28},{5,1},{9... | collective-permute-start | bytes 210440 | tf_op jit(solution)/shard_map/ppermute | solution.py:19
  265.4 13.5 %collective-permute-start.32 = (f32[137,8,128]{2,1,0:T(8,128)S(1)}, f32[137,8,128]{2,1,0:T(8,128)}, u32[]{:S(2)}, u32[]{:S(2)}) collective-permute-start(f32[137,8,128]{2,1,0:T(8,128)S(1)} %copy.219), channel_id=1, source_target_pairs={{0,16},{4,20},{8,24},{12,28},{16,0},{20,4},{24,8},{28,12},{1,17},{... | collective-permute-start | bytes 1683464 | tf_op jit(solution)/shard_map/ppermute | solution.py:25
  265.5 18.4 %collective-permute-start.33 = (f32[137,4,128]{2,0,1:T(8,128)S(1)}, f32[137,4,128]{2,0,1:T(8,128)}, u32[]{:S(2)}, u32[]{:S(2)}) collective-permute-start(f32[137,4,128]{2,0,1:T(8,128)S(1)} %convolution_bitcast_fusion.3), channel_id=1, source_target_pairs={{0,1},{1,2},{2,3},{4,5},{5,6},{6,7},{8,9},{9,10},{10,11},{12,13},{... | collective-permute-start | bytes 841736 | tf_op jit(solution)/shard_map/ppermute | solution.py:16
  269.9 14.0 %collective-permute-start.34 = (f32[137,4,128]{2,0,1:T(8,128)S(1)}, f32[137,4,128]{2,0,1:T(8,128)S(1)}, u32[]{:S(2)}, u32[]{:S(2)}) collective-permute-start(f32[137,4,128]{2,0,1:T(8,128)S(1)} %convolution_bitcast_fusion.3), channel_id=1, source_target_pairs={{1,0},{2,1},{3,2},{5,4},{6,5},{7,6},{9,8},{10,9},{11,10},{13,12},{... | collective-permute-start | bytes 841736 | tf_op jit(solution)/shard_map/ppermute | solution.py:19
  283.9 1.0 copy-start.7
  289.5 13.5 %collective-permute-start.35 = (f32[137,8,128]{2,1,0:T(8,128)S(1)}, f32[137,8,128]{2,1,0:T(8,128)}, u32[]{:S(2)}, u32[]{:S(2)}) collective-permute-start(f32[137,8,128]{2,1,0:T(8,128)S(1)} %copy.224), channel_id=1, source_target_pairs={{0,16},{4,20},{8,24},{12,28},{16,0},{20,4},{24,8},{28,12},{1,17},{... | collective-permute-start | bytes 1683464 | tf_op jit(solution)/shard_map/ppermute | solution.py:25
  290.9 17.2 %collective-permute-start.36 = (f32[137,4,128]{2,0,1:T(8,128)S(1)}, f32[137,4,128]{2,0,1:T(8,128)}, u32[]{:S(2)}, u32[]{:S(2)}) collective-permute-start(f32[137,4,128]{2,0,1:T(8,128)S(1)} %convolution_bitcast_fusion.1), channel_id=1, source_target_pairs={{0,1},{1,2},{2,3},{4,5},{5,6},{6,7},{8,9},{9,10},{10,11},{12,13},{... | collective-permute-start | bytes 841736 | tf_op jit(solution)/shard_map/ppermute | solution.py:16
  295.8 12.3 %collective-permute-start.37 = (f32[137,4,128]{2,0,1:T(8,128)S(1)}, f32[137,4,128]{2,0,1:T(8,128)S(1)}, u32[]{:S(2)}, u32[]{:S(2)}) collective-permute-start(f32[137,4,128]{2,0,1:T(8,128)S(1)} %convolution_bitcast_fusion.1), channel_id=1, source_target_pairs={{1,0},{2,1},{3,2},{5,4},{6,5},{7,6},{9,8},{10,9},{11,10},{13,12},{... | collective-permute-start | bytes 841736 | tf_op jit(solution)/shard_map/ppermute | solution.py:19
  311.7 8.1 %collective-permute-start.38 = (f32[137,4,32]{2,0,1:T(8,128)S(1)}, f32[137,4,32]{2,0,1:T(8,128)S(1)}, u32[]{:S(2)}, u32[]{:S(2)}) collective-permute-start(f32[137,4,32]{2,0,1:T(8,128)S(1)} %get-tuple-element.48), channel_id=1, source_target_pairs={{0,4},{4,8},{8,12},{12,16},{16,20},{20,24},{24,28},{28,0},{1,5},{5... | collective-permute-start | bytes 210440 | tf_op jit(solution)/shard_map/ppermute | solution.py:16
  311.8 8.5 %collective-permute-start.39 = (f32[137,4,32]{2,0,1:T(8,128)S(1)}, f32[137,4,32]{2,0,1:T(8,128)S(1)}, u32[]{:S(2)}, u32[]{:S(2)}) collective-permute-start(f32[137,4,32]{2,0,1:T(8,128)S(1)} %get-tuple-element.49), channel_id=1, source_target_pairs={{4,0},{8,4},{12,8},{16,12},{20,16},{24,20},{28,24},{0,28},{5,1},{9... | collective-permute-start | bytes 210440 | tf_op jit(solution)/shard_map/ppermute | solution.py:19
where the time goes:
time: 376 us; the launch traced here: 374 us
  waiting for transfers between devices  111 us (30%)
  blocking collectives  83.7 us (22%)
  starting transfers between devices  80.1 us (21%)
  local copies, waits for them, and re-layouts  29.5 us (8%)
  matrix products  29.1 us (8%)
  other arithmetic  23 us (6%)
  between operations  18 us (5%)
    psum x2, blocking collectives, per_device(): lax.psum((jnp.sum(residual * residual), jnp.sum(residual * first), jnp.su...  83.7 us
    ppermute x8, waiting for transfers between devices, from_partner(): lax.ppermute(value, axis, [(i, i ^ 1 << distance) for i in range(lax.axis...  58.4 us
    ppermute x16, waiting for transfers between devices, extended_2(): lax.ppermute(lax.slice_in_dim(block, block.shape[dim] - width, None, axis...  46.3 us
    ppermute x16, starting transfers between devices, extended_2(): lax.ppermute(lax.slice_in_dim(block, block.shape[dim] - width, None, axis...  38.2 us
    ppermute x16, starting transfers between devices, extended_2(): lax.ppermute(lax.slice_in_dim(block, 0, width, axis=dim), axis, backward)  31.9 us
    dot_general x4, matrix products, hessian(): jnp.einsum('kl,lji->kji', vertical_map, forward, precision=lax.Precision....  16.8 us
    gather x16, local copies, waits for them, and re-layouts, merid_apply(): mirrored = jnp.take(polar, mirror_local, axis=2)  16 us
    add x4, other arithmetic, merid_apply(): result = result + weights[offset] * (upper + lower)  13.7 us
  transfers between devices with their start and end apart: 40, of which 21 were waited for; matrix products, arithmetic and copies ran while one was open for 7% of the time, Pallas kernels for 0%

commit v1 on v0

--- a/solution.py
+++ b/solution.py
@@ -111,8 +111,11 @@
     for outer in range(OUTER):
         first = hessian(residual)
         sum_rr, sum_rf, sum_ff = lax.psum(
-            (jnp.sum(residual * residual), jnp.sum(residual * first), jnp.sum(first * first)),
-            ("lon", "lat"),
+            lax.psum(
+                (jnp.sum(residual * residual), jnp.sum(residual * first), jnp.sum(first * first)),
+                "lat",
+            ),
+            "lon",
         )
         second = hessian(first)
         sum_fs = lax.psum(jnp.sum(first * second), ("lon", "lat"))

time: 376 us -> 419 us (1.11)
  blocking collectives: 83.7 us -> 126 us
    psum x0 -> x4, blocking collectives: none -> 103 us  [the longest x2 76.8 us: per_device(): sum_fs = lax.psum(jnp.sum(first * second), ('lon', 'lat'))]
    psum x2, blocking collectives: 83.7 us -> 23.8 us  [per_device(): lax.psum((jnp.sum(residual * residual), jnp.sum(residual * first), jnp.su...]
  transfers between devices with their start and end apart: 40 -> 40, of which waited for: 21 -> 20; matrix products, arithmetic and copies ran while one was open for 7% -> 7% of each run, Pallas kernels for 0% -> 0%
where the time goes in v1:
time: 419 us; the launch traced here: 417 us
  blocking collectives  126 us (30%)
  waiting for transfers between devices  109 us (26%)
  starting transfers between devices  83.5 us (20%)
  local copies, waits for them, and re-layouts  30.4 us (7%)
  matrix products  28.3 us (7%)
  other arithmetic  21.3 us (5%)
  between operations  18.1 us (4%)
    psum x2, blocking collectives, per_device(): sum_fs = lax.psum(jnp.sum(first * second), ('lon', 'lat'))  76.8 us
    ppermute x8, waiting for transfers between devices, from_partner(): lax.ppermute(value, axis, [(i, i ^ 1 << distance) for i in range(lax.axis...  54.9 us
    ppermute x16, waiting for transfers between devices, extended_2(): lax.ppermute(lax.slice_in_dim(block, block.shape[dim] - width, None, axis...  47.7 us
    ppermute x16, starting transfers between devices, extended_2(): lax.ppermute(lax.slice_in_dim(block, block.shape[dim] - width, None, axis...  41.4 us
    ppermute x16, starting transfers between devices, extended_2(): lax.ppermute(lax.slice_in_dim(block, 0, width, axis=dim), axis, backward)  32 us
    psum x2, blocking collectives, per_device(): lax.psum(lax.psum((jnp.sum(residual * residual), jnp.sum(residual * first...  25.7 us
    psum x2, blocking collectives, per_device(): lax.psum((jnp.sum(residual * residual), jnp.sum(residual * first), jnp.su...  23.8 us
    dot_general x4, matrix products, hessian(): jnp.einsum('kl,lji->kji', vertical_map, forward, precision=lax.Precision....  16 us
  transfers between devices with their start and end apart: 40, of which 20 were waited for; matrix products, arithmetic and copies ran while one was open for 7% of the time, Pallas kernels for 0%

profile of v1, /device:TPU:0, one launch (start us, length us, event | category | flops | bytes accessed | tf_op | source)
XLA Modules:
  0.0 416.6 jit_solution(2894125785209538530)
XLA Ops:
  2.3 2.9 collective-permute-start.1
  8.6 1.5 collective-permute-done
  10.1 1.5 collective-permute-done.1
  12.7 2.7 collective-permute-start.2
  16.1 3.5 collective-permute-start.3
  20.9 7.8 %collective-permute-done.2 = f32[137,8,128]{2,1,0:T(8,128)S(1)} collective-permute-done((f32[137,8,128]{2,1,0:T(8,128)S(1)}, f32[137,8,128]{2,1,0:T(8,128)S(1)}, u32[]{:S(2)}, u32[]{:S(2)}) %collective-permute-start.2) | collective-permute-done | bytes 561184 | tf_op jit(solution)/shard_map/ppermute | solution.py:25
  31.5 3.7 fusion.5
  36.8 4.7 %collective-permute-start.6 = (f32[137,4,128]{2,0,1:T(8,128)S(1)}, f32[137,4,128]{2,0,1:T(8,128)}, u32[]{:S(2)}, u32[]{:S(2)}) collective-permute-start(f32[137,4,128]{2,0,1:T(8,128)S(1)} %convolution_bitcast_fusion.13), channel_id=1, source_target_pairs={{0,1},{1,2},{2,3},{4,5},{5,6},{6,7},{8,9},{9,10},{10,11},{12,13},{... | collective-permute-start | bytes 841736 | tf_op jit(solution)/shard_map/ppermute | solution.py:16
  42.8 8.2 %collective-permute-done.5 = f32[137,8,128]{2,1,0:T(8,128)S(1)} collective-permute-done((f32[137,8,128]{2,1,0:T(8,128)S(1)}, f32[137,8,128]{2,1,0:T(8,128)S(1)}, u32[]{:S(2)}, u32[]{:S(2)}) %collective-permute-start.5) | collective-permute-done | bytes 561184 | tf_op jit(solution)/shard_map/ppermute | solution.py:25
  53.0 3.3 fusion.139
  56.5 2.6 collective-permute-start.9
  59.1 7.2 %collective-permute-done.8 = f32[137,4,32]{2,0,1:T(8,128)S(1)} collective-permute-done((f32[137,4,32]{2,0,1:T(8,128)S(1)}, f32[137,4,32]{2,0,1:T(8,128)S(1)}, u32[]{:S(2)}, u32[]{:S(2)}) %collective-permute-start.8) | collective-permute-done | bytes 70176 | tf_op jit(solution)/shard_map/ppermute | solution.py:16
  67.4 2.6 collective-permute-start.11
  70.0 7.1 %collective-permute-done.10 = f32[137,4,32]{2,0,1:T(8,128)S(1)} collective-permute-done((f32[137,4,32]{2,0,1:T(8,128)S(1)}, f32[137,4,32]{2,0,1:T(8,128)S(1)}, u32[]{:S(2)}, u32[]{:S(2)}) %collective-permute-start.10) | collective-permute-done | bytes 70176 | tf_op jit(solution)/shard_map/ppermute | solution.py:16
  78.2 5.1 %collective-permute-start.13 = (f32[137,4,128]{2,0,1:T(8,128)S(1)}, f32[137,4,128]{2,0,1:T(8,128)}, u32[]{:S(2)}, u32[]{:S(2)}) collective-permute-start(f32[137,4,128]{2,0,1:T(8,128)S(1)} %convolution_bitcast_fusion.11), channel_id=1, source_target_pairs={{0,1},{1,2},{2,3},{4,5},{5,6},{6,7},{8,9},{9,10},{10,11},{12,13},{... | collective-permute-start | bytes 841736 | tf_op jit(solution)/shard_map/ppermute | solution.py:16
  84.9 6.2 %collective-permute-done.12 = f32[137,8,128]{2,1,0:T(8,128)S(1)} collective-permute-done((f32[137,8,128]{2,1,0:T(8,128)S(1)}, f32[137,8,128]{2,1,0:T(8,128)S(1)}, u32[]{:S(2)}, u32[]{:S(2)}) %collective-permute-start.12) | collective-permute-done | bytes 561184 | tf_op jit(solution)/shard_map/ppermute | solution.py:25
  94.7 3.7 fusion.4
  100.3 6.2 %collective-permute-start.16 = (f32[137,4,128]{2,0,1:T(8,128)S(1)}, f32[137,4,128]{2,0,1:T(8,128)}, u32[]{:S(2)}, u32[]{:S(2)}) collective-permute-start(f32[137,4,128]{2,0,1:T(8,128)S(1)} %convolution_bitcast_fusion.9), channel_id=1, source_target_pairs={{0,1},{1,2},{2,3},{4,5},{5,6},{6,7},{8,9},{9,10},{10,11},{12,13},{... | collective-permute-start | bytes 841736 | tf_op jit(solution)/shard_map/ppermute | solution.py:16
  107.8 4.7 %collective-permute-done.15 = f32[137,8,128]{2,1,0:T(8,128)S(1)} collective-permute-done((f32[137,8,128]{2,1,0:T(8,128)S(1)}, f32[137,8,128]{2,1,0:T(8,128)S(1)}, u32[]{:S(2)}, u32[]{:S(2)}) %collective-permute-start.15) | collective-permute-done | bytes 561184 | tf_op jit(solution)/shard_map/ppermute | solution.py:25
  114.4 1.7 collective-permute-done.17
  117.1 3.2 fusion.111
  120.5 2.6 collective-permute-start.19
  124.0 6.3 %collective-permute-done.18 = f32[137,4,32]{2,0,1:T(8,128)S(1)} collective-permute-done((f32[137,4,32]{2,0,1:T(8,128)S(1)}, f32[137,4,32]{2,0,1:T(8,128)S(1)}, u32[]{:S(2)}, u32[]{:S(2)}) %collective-permute-start.18) | collective-permute-done | bytes 70176 | tf_op jit(solution)/shard_map/ppermute | solution.py:16
  130.3 1.5 multiply_reduce_fusion.6
  131.8 10.4 %all-reduce.3 = (f32[]{:T(128)}, f32[]{:T(128)}, f32[]{:T(128)}) all-reduce(f32[]{:T(128)} %get-tuple-element.18, f32[]{:T(128)} %get-tuple-element.19, f32[]{:T(128)} %multiply_reduce_fusion.7), channel_id=1, replica_groups=mesh['lon'=8,'lat'=4] {'lat'}, use_global_device_ids=true, to_apply=%region_11.13 | all-reduce | flops 3 | bytes 24 | tf_op jit(solution)/shard_map/psum | solution.py:114
  142.1 13.2 %all-reduce.1 = (f32[]{:T(128)}, f32[]{:T(128)}, f32[]{:T(128)}) all-reduce(f32[]{:T(128)} %get-tuple-element.29, f32[]{:T(128)} %get-tuple-element.30, f32[]{:T(128)} %get-tuple-element.31), channel_id=1, replica_groups=mesh['lon'=8,'lat'=4] {'lon'}, use_global_device_ids=true, to_apply=%region_12.14 | all-reduce | flops 3 | bytes 24 | tf_op jit(solution)/shard_map/psum | solution.py:113
  158.1 39.1 %psum.98 = f32[]{:T(128)} all-reduce(f32[]{:T(128)} %get-tuple-element.17), channel_id=1, replica_groups=mesh['lon'=8,'lat'=4] {'lon','lat'}, use_global_device_ids=true, to_apply=%region_3.5 | all-reduce | flops 1 | bytes 8 | tf_op jit(solution)/shard_map/psum | solution.py:121
  202.9 2.6 collective-permute-start.21
  205.6 4.4 %collective-permute-done.20 = f32[137,4,32]{2,0,1:T(8,128)S(1)} collective-permute-done((f32[137,4,32]{2,0,1:T(8,128)S(1)}, f32[137,4,32]{2,0,1:T(8,128)S(1)}, u32[]{:S(2)}, u32[]{:S(2)}) %collective-permute-start.20) | collective-permute-done | bytes 70176 | tf_op jit(solution)/shard_map/ppermute | solution.py:16
  210.0 2.1 collective-permute-done.21
  212.0 1.5 convolution_bitcast_fusion.7
  214.8 3.2 collective-permute-start.22
  218.0 4.1 collective-permute-start.23
  223.4 8.1 %collective-permute-done.22 = f32[137,8,128]{2,1,0:T(8,128)S(1)} collective-permute-done((f32[137,8,128]{2,1,0:T(8,128)S(1)}, f32[137,8,128]{2,1,0:T(8,128)S(1)}, u32[]{:S(2)}, u32[]{:S(2)}) %collective-permute-start.22) | collective-permute-done | bytes 561184 | tf_op jit(solution)/shard_map/ppermute | solution.py:25
  234.5 5.1 %fusion.3 = f32[137,4,128]{2,0,1:T(8,128)S(1)} fusion(f32[137,4,128]{2,0,1:T(8,128)S(1)} %reverse_select_fusion.6, f32[137,4,128]{2,0,1:T(8,128)S(1)} %reverse_select_fusion.7, f32[137,4,128]{2,0,1:T(8,128)} %convolution_bitcast_fusion.7, f32[137,4,128]{2,1,0:T(4,128)S(1)} %copy-done.6, f32[137,137]{1,0:T(8,128)S(1)} %copy-done, f32[]{:T(128)} %bitcast.9, ...), kind=kOutput, calls=%fused_computation.19 | convolution fusion | flops 116719616 | bytes 1477976 | tf_op jit(solution)/shard_map/kl,lji->kji/dot_general | solution.py:100
  240.8 5.0 %collective-permute-start.26 = (f32[137,4,128]{2,0,1:T(8,128)S(1)}, f32[137,4,128]{2,0,1:T(8,128)}, u32[]{:S(2)}, u32[]{:S(2)}) collective-permute-start(f32[137,4,128]{2,0,1:T(8,128)S(1)} %convolution_bitcast_fusion.5), channel_id=1, source_target_pairs={{0,1},{1,2},{2,3},{4,5},{5,6},{6,7},{8,9},{9,10},{10,11},{12,13},{... | collective-permute-start | bytes 841736 | tf_op jit(solution)/shard_map/ppermute | solution.py:16
  245.8 1.5 collective-permute-start.27
  247.3 7.9 %collective-permute-done.25 = f32[137,8,128]{2,1,0:T(8,128)S(1)} collective-permute-done((f32[137,8,128]{2,1,0:T(8,128)S(1)}, f32[137,8,128]{2,1,0:T(8,128)S(1)}, u32[]{:S(2)}, u32[]{:S(2)}) %collective-permute-start.25) | collective-permute-done | bytes 561184 | tf_op jit(solution)/shard_map/ppermute | solution.py:25
  255.8 1.7 gather_fusion.5
  257.5 1.6 copy.216
  260.3 3.2 fusion.83
  263.7 2.6 collective-permute-start.29
  266.4 6.5 %collective-permute-done.28 = f32[137,4,32]{2,0,1:T(8,128)S(1)} collective-permute-done((f32[137,4,32]{2,0,1:T(8,128)S(1)}, f32[137,4,32]{2,0,1:T(8,128)S(1)}, u32[]{:S(2)}, u32[]{:S(2)}) %collective-permute-start.28) | collective-permute-done | bytes 70176 | tf_op jit(solution)/shard_map/ppermute | solution.py:16
  273.9 2.6 collective-permute-start.31
  276.6 7.4 %collective-permute-done.30 = f32[137,4,32]{2,0,1:T(8,128)S(1)} collective-permute-done((f32[137,4,32]{2,0,1:T(8,128)S(1)}, f32[137,4,32]{2,0,1:T(8,128)S(1)}, u32[]{:S(2)}, u32[]{:S(2)}) %collective-permute-start.30) | collective-permute-done | bytes 70176 | tf_op jit(solution)/shard_map/ppermute | solution.py:16
  285.1 5.9 %collective-permute-start.33 = (f32[137,4,128]{2,0,1:T(8,128)S(1)}, f32[137,4,128]{2,0,1:T(8,128)}, u32[]{:S(2)}, u32[]{:S(2)}) collective-permute-start(f32[137,4,128]{2,0,1:T(8,128)S(1)} %convolution_bitcast_fusion.3), channel_id=1, source_target_pairs={{0,1},{1,2},{2,3},{4,5},{5,6},{6,7},{8,9},{9,10},{10,11},{12,13},{... | collective-permute-start | bytes 841736 | tf_op jit(solution)/shard_map/ppermute | solution.py:16
  292.3 6.4 %collective-permute-done.32 = f32[137,8,128]{2,1,0:T(8,128)} collective-permute-done((f32[137,8,128]{2,1,0:T(8,128)S(1)}, f32[137,8,128]{2,1,0:T(8,128)}, u32[]{:S(2)}, u32[]{:S(2)}) %collective-permute-start.32) | collective-permute-done | bytes 561184 | tf_op jit(solution)/shard_map/ppermute | solution.py:25
  298.6 1.6 copy.220
  300.2 1.7 gather_fusion.6
  302.0 1.6 copy.221
  304.6 3.7 fusion.2
  309.1 1.8 collective-permute-start.35
  310.9 6.0 %collective-permute-start.36 = (f32[137,4,128]{2,0,1:T(8,128)S(1)}, f32[137,4,128]{2,0,1:T(8,128)}, u32[]{:S(2)}, u32[]{:S(2)}) collective-permute-start(f32[137,4,128]{2,0,1:T(8,128)S(1)} %convolution_bitcast_fusion.1), channel_id=1, source_target_pairs={{0,1},{1,2},{2,3},{4,5},{5,6},{6,7},{8,9},{9,10},{10,11},{12,13},{... | collective-permute-start | bytes 841736 | tf_op jit(solution)/shard_map/ppermute | solution.py:16
  318.2 5.4 %collective-permute-done.35 = f32[137,8,128]{2,1,0:T(8,128)} collective-permute-done((f32[137,8,128]{2,1,0:T(8,128)S(1)}, f32[137,8,128]{2,1,0:T(8,128)}, u32[]{:S(2)}, u32[]{:S(2)}) %collective-permute-start.35) | collective-permute-done | bytes 561184 | tf_op jit(solution)/shard_map/ppermute | solution.py:25
  323.7 1.6 copy.225
  325.2 1.7 gather_fusion.7
  327.0 1.6 copy.226
  328.8 3.2 fusion.55
  332.2 2.6 collective-permute-start.39
  334.8 7.3 %collective-permute-done.38 = f32[137,4,32]{2,0,1:T(8,128)S(1)} collective-permute-done((f32[137,4,32]{2,0,1:T(8,128)S(1)}, f32[137,4,32]{2,0,1:T(8,128)S(1)}, u32[]{:S(2)}, u32[]{:S(2)}) %collective-permute-start.38) | collective-permute-done | bytes 70176 | tf_op jit(solution)/shard_map/ppermute | solution.py:16
  342.1 1.5 multiply_reduce_fusion.3
  343.6 13.5 %all-reduce.2 = (f32[]{:T(128)}, f32[]{:T(128)}, f32[]{:T(128)}) all-reduce(f32[]{:T(128)} %get-tuple-element.14, f32[]{:T(128)} %get-tuple-element.16, f32[]{:T(128)} %get-tuple-element.15), channel_id=1, replica_groups=mesh['lon'=8,'lat'=4] {'lat'}, use_global_device_ids=true, to_apply=%region_22.24 | all-reduce | flops 3 | bytes 24 | tf_op jit(solution)/shard_map/psum | solution.py:114
  357.1 12.5 %all-reduce = (f32[]{:T(128)}, f32[]{:T(128)}, f32[]{:T(128)}) all-reduce(f32[]{:T(128)} %get-tuple-element.26, f32[]{:T(128)} %get-tuple-element.27, f32[]{:T(128)} %get-tuple-element.28), channel_id=1, replica_groups=mesh['lon'=8,'lat'=4] {'lon'}, use_global_device_ids=true, to_apply=%region_23.25 | all-reduce | flops 3 | bytes 24 | tf_op jit(solution)/shard_map/psum | solution.py:113
  371.9 37.7 %psum.105 = f32[]{:T(128)} all-reduce(f32[]{:T(128)} %get-tuple-element.13), channel_id=1, replica_groups=mesh['lon'=8,'lat'=4] {'lon','lat'}, use_global_device_ids=true, to_apply=%region_14.16 | all-reduce | flops 1 | bytes 8 | tf_op jit(solution)/shard_map/psum | solution.py:121
  (161 shorter events, 46.6 us)
Async XLA Ops:
  0.6 30.1 %copy-start = (f32[137,137]{1,0:T(8,128)S(1)}, f32[137,137]{1,0:T(8,128)}, u32[]{:S(2)}) copy-start(f32[137,137]{1,0:T(8,128)} %param.15) | copy-start | bytes 225232
  0.6 4.6 %copy-start.3 = (s32[4]{0:T(128)S(1)}, s32[4]{0:T(128)}, u32[]{:S(2)}) copy-start(s32[4]{0:T(128)} %param.11) | copy-start | bytes 52
  0.7 4.6 %copy-start.2 = (f32[4,33]{1,0:T(4,128)S(1)}, f32[4,33]{1,0:T(4,128)}, u32[]{:S(2)}) copy-start(f32[4,33]{1,0:T(4,128)} %param.12) | copy-start | bytes 1588
  0.7 5.2 %copy-start.9 = (f32[5]{0:T(128)S(1)}, f32[5]{0:T(128)}, u32[]{:S(2)}) copy-start(f32[5]{0:T(128)} %param.14) | copy-start | bytes 64
  1.8 8.3 %collective-permute-start = (f32[137,4,32]{2,0,1:T(8,128)S(1)}, f32[137,4,32]{2,0,1:T(8,128)S(1)}, u32[]{:S(2)}, u32[]{:S(2)}) collective-permute-start(f32[137,4,32]{2,0,1:T(8,128)S(1)} %get-tuple-element.66), channel_id=1, source_target_pairs={{0,4},{4,8},{8,12},{12,16},{16,20},{20,24},{24,28},{28,0},{1,5},{5... | collective-permute-start | bytes 210440 | tf_op jit(solution)/shard_map/ppermute | solution.py:16
  2.3 9.3 %collective-permute-start.1 = (f32[137,4,32]{2,0,1:T(8,128)S(1)}, f32[137,4,32]{2,0,1:T(8,128)S(1)}, u32[]{:S(2)}, u32[]{:S(2)}) collective-permute-start(f32[137,4,32]{2,0,1:T(8,128)S(1)} %get-tuple-element.67), channel_id=1, source_target_pairs={{4,0},{8,4},{12,8},{16,12},{20,16},{24,20},{28,24},{0,28},{5,1},{9... | collective-permute-start | bytes 210440 | tf_op jit(solution)/shard_map/ppermute | solution.py:19
  12.5 2.9 copy-start.8
  12.7 16.0 %collective-permute-start.2 = (f32[137,8,128]{2,1,0:T(8,128)S(1)}, f32[137,8,128]{2,1,0:T(8,128)S(1)}, u32[]{:S(2)}, u32[]{:S(2)}) collective-permute-start(f32[137,8,128]{2,1,0:T(8,128)S(1)} %copy.185), channel_id=1, source_target_pairs={{0,16},{4,20},{8,24},{12,28},{16,0},{20,4},{24,8},{28,12},{1,17},{... | collective-permute-start | bytes 1683464 | tf_op jit(solution)/shard_map/ppermute | solution.py:25
  16.1 14.5 %collective-permute-start.3 = (f32[137,4,128]{2,0,1:T(8,128)S(1)}, f32[137,4,128]{2,0,1:T(8,128)S(1)}, u32[]{:S(2)}, u32[]{:S(2)}) collective-permute-start(f32[137,4,128]{2,0,1:T(8,128)S(1)} %convolution_bitcast_fusion.15), channel_id=1, source_target_pairs={{0,1},{1,2},{2,3},{4,5},{5,6},{6,7},{8,9},{9,10},{10,11},{12,13},{... | collective-permute-start | bytes 841736 | tf_op jit(solution)/shard_map/ppermute | solution.py:16
  19.6 11.0 %collective-permute-start.4 = (f32[137,4,128]{2,0,1:T(8,128)S(1)}, f32[137,4,128]{2,0,1:T(8,128)S(1)}, u32[]{:S(2)}, u32[]{:S(2)}) collective-permute-start(f32[137,4,128]{2,0,1:T(8,128)S(1)} %convolution_bitcast_fusion.15), channel_id=1, source_target_pairs={{1,0},{2,1},{3,2},{5,4},{6,5},{7,6},{9,8},{10,9},{11,10},{13,12},{... | collective-permute-start | bytes 841736 | tf_op jit(solution)/shard_map/ppermute | solution.py:19
  30.6 1.0 copy-start.4
  36.0 15.0 %collective-permute-start.5 = (f32[137,8,128]{2,1,0:T(8,128)S(1)}, f32[137,8,128]{2,1,0:T(8,128)S(1)}, u32[]{:S(2)}, u32[]{:S(2)}) collective-permute-start(f32[137,8,128]{2,1,0:T(8,128)S(1)} %copy.190), channel_id=1, source_target_pairs={{0,16},{4,20},{8,24},{12,28},{16,0},{20,4},{24,8},{28,12},{1,17},{... | collective-permute-start | bytes 1683464 | tf_op jit(solution)/shard_map/ppermute | solution.py:25
  36.8 16.1 %collective-permute-start.6 = (f32[137,4,128]{2,0,1:T(8,128)S(1)}, f32[137,4,128]{2,0,1:T(8,128)}, u32[]{:S(2)}, u32[]{:S(2)}) collective-permute-start(f32[137,4,128]{2,0,1:T(8,128)S(1)} %convolution_bitcast_fusion.13), channel_id=1, source_target_pairs={{0,1},{1,2},{2,3},{4,5},{5,6},{6,7},{8,9},{9,10},{10,11},{12,13},{... | collective-permute-start | bytes 841736 | tf_op jit(solution)/shard_map/ppermute | solution.py:16
  41.5 11.4 %collective-permute-start.7 = (f32[137,4,128]{2,0,1:T(8,128)S(1)}, f32[137,4,128]{2,0,1:T(8,128)S(1)}, u32[]{:S(2)}, u32[]{:S(2)}) collective-permute-start(f32[137,4,128]{2,0,1:T(8,128)S(1)} %convolution_bitcast_fusion.13), channel_id=1, source_target_pairs={{1,0},{2,1},{3,2},{5,4},{6,5},{7,6},{9,8},{10,9},{11,10},{13,12},{... | collective-permute-start | bytes 841736 | tf_op jit(solution)/shard_map/ppermute | solution.py:19
  53.0 13.3 %copy-start.1 = (f32[137,4,128]{2,1,0:T(4,128)S(1)}, f32[137,4,128]{2,1,0:T(4,128)}, u32[]{:S(2)}) copy-start(f32[137,4,128]{2,1,0:T(4,128)} %param.9) | copy-start | bytes 841732
  56.4 9.9 %collective-permute-start.8 = (f32[137,4,32]{2,0,1:T(8,128)S(1)}, f32[137,4,32]{2,0,1:T(8,128)S(1)}, u32[]{:S(2)}, u32[]{:S(2)}) collective-permute-start(f32[137,4,32]{2,0,1:T(8,128)S(1)} %get-tuple-element.64), channel_id=1, source_target_pairs={{0,4},{4,8},{8,12},{12,16},{16,20},{20,24},{24,28},{28,0},{1,5},{5... | collective-permute-start | bytes 210440 | tf_op jit(solution)/shard_map/ppermute | solution.py:16
  56.5 9.8 %collective-permute-start.9 = (f32[137,4,32]{2,0,1:T(8,128)S(1)}, f32[137,4,32]{2,0,1:T(8,128)S(1)}, u32[]{:S(2)}, u32[]{:S(2)}) collective-permute-start(f32[137,4,32]{2,0,1:T(8,128)S(1)} %get-tuple-element.65), channel_id=1, source_target_pairs={{4,0},{8,4},{12,8},{16,12},{20,16},{24,20},{28,24},{0,28},{5,1},{9... | collective-permute-start | bytes 210440 | tf_op jit(solution)/shard_map/ppermute | solution.py:19
  67.3 9.8 %collective-permute-start.10 = (f32[137,4,32]{2,0,1:T(8,128)S(1)}, f32[137,4,32]{2,0,1:T(8,128)S(1)}, u32[]{:S(2)}, u32[]{:S(2)}) collective-permute-start(f32[137,4,32]{2,0,1:T(8,128)S(1)} %get-tuple-element.62), channel_id=1, source_target_pairs={{0,4},{4,8},{8,12},{12,16},{16,20},{20,24},{24,28},{28,0},{1,5},{5... | collective-permute-start | bytes 210440 | tf_op jit(solution)/shard_map/ppermute | solution.py:16
  67.4 9.7 %collective-permute-start.11 = (f32[137,4,32]{2,0,1:T(8,128)S(1)}, f32[137,4,32]{2,0,1:T(8,128)S(1)}, u32[]{:S(2)}, u32[]{:S(2)}) collective-permute-start(f32[137,4,32]{2,0,1:T(8,128)S(1)} %get-tuple-element.63), channel_id=1, source_target_pairs={{4,0},{8,4},{12,8},{16,12},{20,16},{24,20},{28,24},{0,28},{5,1},{9... | collective-permute-start | bytes 210440 | tf_op jit(solution)/shard_map/ppermute | solution.py:19
  78.2 12.9 %collective-permute-start.12 = (f32[137,8,128]{2,1,0:T(8,128)S(1)}, f32[137,8,128]{2,1,0:T(8,128)S(1)}, u32[]{:S(2)}, u32[]{:S(2)}) collective-permute-start(f32[137,8,128]{2,1,0:T(8,128)S(1)} %copy.196), channel_id=1, source_target_pairs={{0,16},{4,20},{8,24},{12,28},{16,0},{20,4},{24,8},{28,12},{1,17},{... | collective-permute-start | bytes 1683464 | tf_op jit(solution)/shard_map/ppermute | solution.py:25
  78.2 14.7 %collective-permute-start.13 = (f32[137,4,128]{2,0,1:T(8,128)S(1)}, f32[137,4,128]{2,0,1:T(8,128)}, u32[]{:S(2)}, u32[]{:S(2)}) collective-permute-start(f32[137,4,128]{2,0,1:T(8,128)S(1)} %convolution_bitcast_fusion.11), channel_id=1, source_target_pairs={{0,1},{1,2},{2,3},{4,5},{5,6},{6,7},{8,9},{9,10},{10,11},{12,13},{... | collective-permute-start | bytes 841736 | tf_op jit(solution)/shard_map/ppermute | solution.py:16
  83.4 10.3 %collective-permute-start.14 = (f32[137,4,128]{2,0,1:T(8,128)S(1)}, f32[137,4,128]{2,0,1:T(8,128)}, u32[]{:S(2)}, u32[]{:S(2)}) collective-permute-start(f32[137,4,128]{2,0,1:T(8,128)S(1)} %convolution_bitcast_fusion.11), channel_id=1, source_target_pairs={{1,0},{2,1},{3,2},{5,4},{6,5},{7,6},{9,8},{10,9},{11,10},{13,12},{... | collective-permute-start | bytes 841736 | tf_op jit(solution)/shard_map/ppermute | solution.py:19
  92.9 1.8 copy-start.5
  99.2 13.2 %collective-permute-start.15 = (f32[137,8,128]{2,1,0:T(8,128)S(1)}, f32[137,8,128]{2,1,0:T(8,128)S(1)}, u32[]{:S(2)}, u32[]{:S(2)}) collective-permute-start(f32[137,8,128]{2,1,0:T(8,128)S(1)} %copy.201), channel_id=1, source_target_pairs={{0,16},{4,20},{8,24},{12,28},{16,0},{20,4},{24,8},{28,12},{1,17},{... | collective-permute-start | bytes 1683464 | tf_op jit(solution)/shard_map/ppermute | solution.py:25
  100.3 14.0 %collective-permute-start.16 = (f32[137,4,128]{2,0,1:T(8,128)S(1)}, f32[137,4,128]{2,0,1:T(8,128)}, u32[]{:S(2)}, u32[]{:S(2)}) collective-permute-start(f32[137,4,128]{2,0,1:T(8,128)S(1)} %convolution_bitcast_fusion.9), channel_id=1, source_target_pairs={{0,1},{1,2},{2,3},{4,5},{5,6},{6,7},{8,9},{9,10},{10,11},{12,13},{... | collective-permute-start | bytes 841736 | tf_op jit(solution)/shard_map/ppermute | solution.py:16
  106.5 9.6 %collective-permute-start.17 = (f32[137,4,128]{2,0,1:T(8,128)S(1)}, f32[137,4,128]{2,0,1:T(8,128)}, u32[]{:S(2)}, u32[]{:S(2)}) collective-permute-start(f32[137,4,128]{2,0,1:T(8,128)S(1)} %convolution_bitcast_fusion.9), channel_id=1, source_target_pairs={{1,0},{2,1},{3,2},{5,4},{6,5},{7,6},{9,8},{10,9},{11,10},{13,12},{... | collective-permute-start | bytes 841736 | tf_op jit(solution)/shard_map/ppermute | solution.py:19
  120.5 9.8 %collective-permute-start.18 = (f32[137,4,32]{2,0,1:T(8,128)S(1)}, f32[137,4,32]{2,0,1:T(8,128)S(1)}, u32[]{:S(2)}, u32[]{:S(2)}) collective-permute-start(f32[137,4,32]{2,0,1:T(8,128)S(1)} %get-tuple-element.60), channel_id=1, source_target_pairs={{0,4},{4,8},{8,12},{12,16},{16,20},{20,24},{24,28},{28,0},{1,5},{5... | collective-permute-start | bytes 210440 | tf_op jit(solution)/shard_map/ppermute | solution.py:16
  120.5 9.7 %collective-permute-start.19 = (f32[137,4,32]{2,0,1:T(8,128)S(1)}, f32[137,4,32]{2,0,1:T(8,128)S(1)}, u32[]{:S(2)}, u32[]{:S(2)}) collective-permute-start(f32[137,4,32]{2,0,1:T(8,128)S(1)} %get-tuple-element.61), channel_id=1, source_target_pairs={{4,0},{8,4},{12,8},{16,12},{20,16},{24,20},{28,24},{0,28},{5,1},{9... | collective-permute-start | bytes 210440 | tf_op jit(solution)/shard_map/ppermute | solution.py:19
  202.9 7.1 %collective-permute-start.20 = (f32[137,4,32]{2,0,1:T(8,128)S(1)}, f32[137,4,32]{2,0,1:T(8,128)S(1)}, u32[]{:S(2)}, u32[]{:S(2)}) collective-permute-start(f32[137,4,32]{2,0,1:T(8,128)S(1)} %get-tuple-element.58), channel_id=1, source_target_pairs={{0,4},{4,8},{8,12},{12,16},{16,20},{20,24},{24,28},{28,0},{1,5},{5... | collective-permute-start | bytes 210440 | tf_op jit(solution)/shard_map/ppermute | solution.py:16
  202.9 9.1 %collective-permute-start.21 = (f32[137,4,32]{2,0,1:T(8,128)S(1)}, f32[137,4,32]{2,0,1:T(8,128)S(1)}, u32[]{:S(2)}, u32[]{:S(2)}) collective-permute-start(f32[137,4,32]{2,0,1:T(8,128)S(1)} %get-tuple-element.59), channel_id=1, source_target_pairs={{4,0},{8,4},{12,8},{16,12},{20,16},{24,20},{28,24},{0,28},{5,1},{9... | collective-permute-start | bytes 210440 | tf_op jit(solution)/shard_map/ppermute | solution.py:19
  214.8 16.7 %collective-permute-start.22 = (f32[137,8,128]{2,1,0:T(8,128)S(1)}, f32[137,8,128]{2,1,0:T(8,128)S(1)}, u32[]{:S(2)}, u32[]{:S(2)}) collective-permute-start(f32[137,8,128]{2,1,0:T(8,128)S(1)} %copy.209), channel_id=1, source_target_pairs={{0,16},{4,20},{8,24},{12,28},{16,0},{20,4},{24,8},{28,12},{1,17},{... | collective-permute-start | bytes 1683464 | tf_op jit(solution)/shard_map/ppermute | solution.py:25
  218.0 15.4 %collective-permute-start.23 = (f32[137,4,128]{2,0,1:T(8,128)}, f32[137,4,128]{2,0,1:T(8,128)}, u32[]{:S(2)}, u32[]{:S(2)}) collective-permute-start(f32[137,4,128]{2,0,1:T(8,128)} %convolution_bitcast_fusion.7), channel_id=1, source_target_pairs={{0,1},{1,2},{2,3},{4,5},{5,6},{6,7},{8,9},{9,10},{10,11},{12,13},{... | collective-permute-start | bytes 841736 | tf_op jit(solution)/shard_map/ppermute | solution.py:16
  222.1 11.4 %collective-permute-start.24 = (f32[137,4,128]{2,0,1:T(8,128)}, f32[137,4,128]{2,0,1:T(8,128)}, u32[]{:S(2)}, u32[]{:S(2)}) collective-permute-start(f32[137,4,128]{2,0,1:T(8,128)} %convolution_bitcast_fusion.7), channel_id=1, source_target_pairs={{1,0},{2,1},{3,2},{5,4},{6,5},{7,6},{9,8},{10,9},{11,10},{13,12},{... | collective-permute-start | bytes 841736 | tf_op jit(solution)/shard_map/ppermute | solution.py:19
  233.4 1.1 copy-start.6
  240.4 14.8 %collective-permute-start.25 = (f32[137,8,128]{2,1,0:T(8,128)S(1)}, f32[137,8,128]{2,1,0:T(8,128)S(1)}, u32[]{:S(2)}, u32[]{:S(2)}) collective-permute-start(f32[137,8,128]{2,1,0:T(8,128)S(1)} %copy.214), channel_id=1, source_target_pairs={{0,16},{4,20},{8,24},{12,28},{16,0},{20,4},{24,8},{28,12},{1,17},{... | collective-permute-start | bytes 1683464 | tf_op jit(solution)/shard_map/ppermute | solution.py:25
  240.8 18.4 %collective-permute-start.26 = (f32[137,4,128]{2,0,1:T(8,128)S(1)}, f32[137,4,128]{2,0,1:T(8,128)}, u32[]{:S(2)}, u32[]{:S(2)}) collective-permute-start(f32[137,4,128]{2,0,1:T(8,128)S(1)} %convolution_bitcast_fusion.5), channel_id=1, source_target_pairs={{0,1},{1,2},{2,3},{4,5},{5,6},{6,7},{8,9},{9,10},{10,11},{12,13},{... | collective-permute-start | bytes 841736 | tf_op jit(solution)/shard_map/ppermute | solution.py:16
  245.8 13.5 %collective-permute-start.27 = (f32[137,4,128]{2,0,1:T(8,128)S(1)}, f32[137,4,128]{2,0,1:T(8,128)}, u32[]{:S(2)}, u32[]{:S(2)}) collective-permute-start(f32[137,4,128]{2,0,1:T(8,128)S(1)} %convolution_bitcast_fusion.5), channel_id=1, source_target_pairs={{1,0},{2,1},{3,2},{5,4},{6,5},{7,6},{9,8},{10,9},{11,10},{13,12},{... | collective-permute-start | bytes 841736 | tf_op jit(solution)/shard_map/ppermute | solution.py:19
  263.7 9.2 %collective-permute-start.28 = (f32[137,4,32]{2,0,1:T(8,128)S(1)}, f32[137,4,32]{2,0,1:T(8,128)S(1)}, u32[]{:S(2)}, u32[]{:S(2)}) collective-permute-start(f32[137,4,32]{2,0,1:T(8,128)S(1)} %get-tuple-element.56), channel_id=1, source_target_pairs={{0,4},{4,8},{8,12},{12,16},{16,20},{20,24},{24,28},{28,0},{1,5},{5... | collective-permute-start | bytes 210440 | tf_op jit(solution)/shard_map/ppermute | solution.py:16
  263.7 9.2 %collective-permute-start.29 = (f32[137,4,32]{2,0,1:T(8,128)S(1)}, f32[137,4,32]{2,0,1:T(8,128)S(1)}, u32[]{:S(2)}, u32[]{:S(2)}) collective-permute-start(f32[137,4,32]{2,0,1:T(8,128)S(1)} %get-tuple-element.57), channel_id=1, source_target_pairs={{4,0},{8,4},{12,8},{16,12},{20,16},{24,20},{28,24},{0,28},{5,1},{9... | collective-permute-start | bytes 210440 | tf_op jit(solution)/shard_map/ppermute | solution.py:19
  273.9 10.1 %collective-permute-start.30 = (f32[137,4,32]{2,0,1:T(8,128)S(1)}, f32[137,4,32]{2,0,1:T(8,128)S(1)}, u32[]{:S(2)}, u32[]{:S(2)}) collective-permute-start(f32[137,4,32]{2,0,1:T(8,128)S(1)} %get-tuple-element.54), channel_id=1, source_target_pairs={{0,4},{4,8},{8,12},{12,16},{16,20},{20,24},{24,28},{28,0},{1,5},{5... | collective-permute-start | bytes 210440 | tf_op jit(solution)/shard_map/ppermute | solution.py:16
  273.9 10.0 %collective-permute-start.31 = (f32[137,4,32]{2,0,1:T(8,128)S(1)}, f32[137,4,32]{2,0,1:T(8,128)S(1)}, u32[]{:S(2)}, u32[]{:S(2)}) collective-permute-start(f32[137,4,32]{2,0,1:T(8,128)S(1)} %get-tuple-element.55), channel_id=1, source_target_pairs={{4,0},{8,4},{12,8},{16,12},{20,16},{24,20},{28,24},{0,28},{5,1},{9... | collective-permute-start | bytes 210440 | tf_op jit(solution)/shard_map/ppermute | solution.py:19
  285.0 13.6 %collective-permute-start.32 = (f32[137,8,128]{2,1,0:T(8,128)S(1)}, f32[137,8,128]{2,1,0:T(8,128)}, u32[]{:S(2)}, u32[]{:S(2)}) collective-permute-start(f32[137,8,128]{2,1,0:T(8,128)S(1)} %copy.219), channel_id=1, source_target_pairs={{0,16},{4,20},{8,24},{12,28},{16,0},{20,4},{24,8},{28,12},{1,17},{... | collective-permute-start | bytes 1683464 | tf_op jit(solution)/shard_map/ppermute | solution.py:25
  285.1 18.5 %collective-permute-start.33 = (f32[137,4,128]{2,0,1:T(8,128)S(1)}, f32[137,4,128]{2,0,1:T(8,128)}, u32[]{:S(2)}, u32[]{:S(2)}) collective-permute-start(f32[137,4,128]{2,0,1:T(8,128)S(1)} %convolution_bitcast_fusion.3), channel_id=1, source_target_pairs={{0,1},{1,2},{2,3},{4,5},{5,6},{6,7},{8,9},{9,10},{10,11},{12,13},{... | collective-permute-start | bytes 841736 | tf_op jit(solution)/shard_map/ppermute | solution.py:16
  291.0 12.7 %collective-permute-start.34 = (f32[137,4,128]{2,0,1:T(8,128)S(1)}, f32[137,4,128]{2,0,1:T(8,128)S(1)}, u32[]{:S(2)}, u32[]{:S(2)}) collective-permute-start(f32[137,4,128]{2,0,1:T(8,128)S(1)} %convolution_bitcast_fusion.3), channel_id=1, source_target_pairs={{1,0},{2,1},{3,2},{5,4},{6,5},{7,6},{9,8},{10,9},{11,10},{13,12},{... | collective-permute-start | bytes 841736 | tf_op jit(solution)/shard_map/ppermute | solution.py:19
  303.6 1.0 copy-start.7
  309.1 14.6 %collective-permute-start.35 = (f32[137,8,128]{2,1,0:T(8,128)S(1)}, f32[137,8,128]{2,1,0:T(8,128)}, u32[]{:S(2)}, u32[]{:S(2)}) collective-permute-start(f32[137,8,128]{2,1,0:T(8,128)S(1)} %copy.224), channel_id=1, source_target_pairs={{0,16},{4,20},{8,24},{12,28},{16,0},{20,4},{24,8},{28,12},{1,17},{... | collective-permute-start | bytes 1683464 | tf_op jit(solution)/shard_map/ppermute | solution.py:25
  310.9 17.8 %collective-permute-start.36 = (f32[137,4,128]{2,0,1:T(8,128)S(1)}, f32[137,4,128]{2,0,1:T(8,128)}, u32[]{:S(2)}, u32[]{:S(2)}) collective-permute-start(f32[137,4,128]{2,0,1:T(8,128)S(1)} %convolution_bitcast_fusion.1), channel_id=1, source_target_pairs={{0,1},{1,2},{2,3},{4,5},{5,6},{6,7},{8,9},{9,10},{10,11},{12,13},{... | collective-permute-start | bytes 841736 | tf_op jit(solution)/shard_map/ppermute | solution.py:16
  316.9 11.8 %collective-permute-start.37 = (f32[137,4,128]{2,0,1:T(8,128)S(1)}, f32[137,4,128]{2,0,1:T(8,128)S(1)}, u32[]{:S(2)}, u32[]{:S(2)}) collective-permute-start(f32[137,4,128]{2,0,1:T(8,128)S(1)} %convolution_bitcast_fusion.1), channel_id=1, source_target_pairs={{1,0},{2,1},{3,2},{5,4},{6,5},{7,6},{9,8},{10,9},{11,10},{13,12},{... | collective-permute-start | bytes 841736 | tf_op jit(solution)/shard_map/ppermute | solution.py:19
  332.1 10.0 %collective-permute-start.38 = (f32[137,4,32]{2,0,1:T(8,128)S(1)}, f32[137,4,32]{2,0,1:T(8,128)S(1)}, u32[]{:S(2)}, u32[]{:S(2)}) collective-permute-start(f32[137,4,32]{2,0,1:T(8,128)S(1)} %get-tuple-element.52), channel_id=1, source_target_pairs={{0,4},{4,8},{8,12},{12,16},{16,20},{20,24},{24,28},{28,0},{1,5},{5... | collective-permute-start | bytes 210440 | tf_op jit(solution)/shard_map/ppermute | solution.py:16
  332.2 9.9 %collective-permute-start.39 = (f32[137,4,32]{2,0,1:T(8,128)S(1)}, f32[137,4,32]{2,0,1:T(8,128)S(1)}, u32[]{:S(2)}, u32[]{:S(2)}) collective-permute-start(f32[137,4,32]{2,0,1:T(8,128)S(1)} %get-tuple-element.53), channel_id=1, source_target_pairs={{4,0},{8,4},{12,8},{16,12},{20,16},{24,20},{28,24},{0,28},{5,1},{9... | collective-permute-start | bytes 210440 | tf_op jit(solution)/shard_map/ppermute | solution.py:19
